TPU v7x, 128 devices: a whole 4x4x4 slice. The times are simulated.
128 devices in a mesh: pipe: 2 (over x_lo), dp: 64 (over z, x_hi, y, core).
Axes of the slice: x: 4 (x_hi: 2, x_lo: 2; x = x_hi * 2 + x_lo), y: 4, z: 4, core: 2. Of those that a mesh axis runs over, the one named last changes fastest.
Arguments:
- segment_input: bfloat16 [2, 512, 12288], P('pipe', 'dp'), may hold values from -3000 to 3000, as said below
- norm_gain: float32 [2, 12288], P('pipe'), may hold values from 0.5 to 2
- head_weights: bfloat16 [2, 12288, 64, 384], P('pipe', None, 'dp'), may hold values from -0.04818163 to 0.04818163
- output_weights: bfloat16 [2, 8192, 12288], P('pipe', 'dp'), may hold values from -0.25 to 0.25
Outputs:
- section_outputs: bfloat16 [2, 512, 12288], P('pipe', 'dp')
Inputs may be any that keep to these rules, and one draw needn't show every extreme that they name: `segment_input`: activations of order one to some thousands, rows and features of unlike scales.
All inputs are finite; a program needn't handle non-finite values.
Results may differ from a plain program's by a relative error of at most 0.0083.
Values may be sent and summed in bfloat16 or wider, within the bound.
No kernel may reach another device: no remote copies, remote signals or barrier semaphores. Data moves between devices by JAX's collectives and lax.ppermute only.
A program may use at most 128 MiB of HBM per device.

v0:
```python
import math
import jax
import jax.numpy as jnp
from jax import lax
from jax.sharding import PartitionSpec as P


def from_behind(value, axis, steps):
    count = lax.axis_size(axis)
    pairs = [(source, (source + steps) % count) for source in range(count)]
    return lax.ppermute(value, axis, pairs)


def normalize(section_rows, gain_vector):
    values = section_rows.astype(jnp.float32)
    centre = jnp.mean(values, axis=-1, keepdims=True)
    shifted = values - centre
    spread = jnp.mean(shifted * shifted, axis=-1, keepdims=True)
    return (shifted * lax.rsqrt(spread + 1e-05) * gain_vector).astype(jnp.bfloat16)


def attend(projected, head_size):
    queries = projected[:, :head_size]
    keys_part = projected[:, head_size : 2 * head_size]
    values_part = projected[:, 2 * head_size :].astype(jnp.bfloat16)
    scores = jnp.einsum(
        "qd,kd->qk", queries, keys_part, precision=lax.Precision.HIGHEST
    ) / math.sqrt(head_size)
    length = projected.shape[0]
    causal = jnp.arange(length)[:, None] >= jnp.arange(length)[None, :]
    scores = jnp.where(causal, scores, -1e30)
    largest = jnp.max(scores, axis=-1, keepdims=True)
    weights = jnp.where(causal, jnp.exp(scores - largest), 0.0)
    totals = jnp.sum(weights, axis=-1, keepdims=True)
    probabilities = (weights / totals).astype(jnp.bfloat16)
    return jnp.dot(probabilities, values_part, preferred_element_type=jnp.float32).astype(
        jnp.bfloat16
    )


def shards(segment_input, norm_gain, head_weights, output_weights):
    head_size = output_weights.shape[1]
    normed = normalize(segment_input[0], norm_gain[0])
    head_block = head_weights[0, :, 0, :]
    projected = jnp.dot(
        lax.all_gather(normed, "dp", axis=0, tiled=True),
        head_block,
        preferred_element_type=jnp.float32,
    )
    attended = attend(projected, head_size)
    out_rows = output_weights[0]
    finished = lax.psum_scatter(
        jnp.dot(attended, out_rows, preferred_element_type=jnp.float32),
        "dp",
        scatter_dimension=0,
        tiled=True,
    ).astype(jnp.bfloat16)
    handed = from_behind(finished, "pipe", 1)
    return handed[None]


def solution(mesh):
    placed = (
        P("pipe", "dp", None),
        P("pipe", None),
        P("pipe", None, "dp", None),
        P("pipe", "dp", None),
    )
    return jax.shard_map(
        shards, mesh=mesh, in_specs=placed, out_specs=P("pipe", "dp", None), check_vma=False
    )
```

profile of v0, /device:TPU:0, one launch (start us, length us, event | category | flops | bytes accessed | tf_op | source)
XLA Modules:
  0.0 382.8 jit_solution(5650053508658786681)
XLA Ops:
  6.5 0.0 copy-start
  6.5 0.0 all-gather.2.cloned.1.call-start
  6.5 1.3 convert_reduce_fusion
  7.8 1.2 fusion.15
  9.1 1.7 fusion.17
  10.8 0.0 all-gather.2.cloned.1.call-update
  10.8 0.0 reduce-scatter.2.cloned.1.call-start
  10.9 95.6 %all-gather.2.cloned.1.call-done = bf16[512,12288]{1,0:T(8,128)(2,1)} async-done(((bf16[8,12288]{1,0:T(8,128)(2,1)}), bf16[512,12288]{1,0:T(8,128)(2,1)}) %all-gather.2.cloned.1.call-update) | async-done | bytes 12582928 | tf_op jit(solution)/shard_map/all_gather | solution.py:46
  106.5 12.7 %fusion = f32[512,384]{1,0:T(8,128)S(1)} fusion(bf16[512,12288]{1,0:T(8,128)(2,1)} %all-gather.2.cloned.1.call-done, bf16[1,12288,1,384]{3,1,2,0:T(8,128)(2,1)} %param.6), kind=kOutput, calls=%fused_computation | convolution fusion | flops 4831838208 | bytes 22806528 | tf_op jit(solution)/shard_map/dot_general | solution.py:45
  119.2 0.0 copy-start.2
  119.2 0.9 copy-done.2
  120.1 1.0 fusion.22
  121.1 0.0 copy-start.1
  121.1 1.1 copy-done.1
  122.2 0.2 fusion.5
  122.3 0.0 copy-done
  122.3 11.8 %fusion.2 = f32[512,12288]{1,0:T(8,128)} fusion(bf16[1,128,12288]{2,1,0:T(8,128)(2,1)S(1)} %copy-done, f32[512,512]{0,1:T(8,128)} %copy-done.1, f32[512]{0:T(512)S(1)} %fusion.5, f32[512]{0:T(512)S(1)} %get-tuple-element.5, f32[512,384]{1,0:T(8,128)} %copy-done.2), kind=kOutput, calls=%fused_computation.2 | convolution fusion | flops 1679097856 | bytes 29495296 | tf_op jit(solution)/shard_map/dot_general | solution.py:53
  134.1 0.0 reduce-scatter.2.cloned.1.call-update
  134.1 234.4 %reduce-scatter.2.cloned.1.call-done = f32[8,12288]{1,0:T(8,128)} async-done(((f32[512,12288]{1,0:T(8,128)}), f32[8,12288]{1,0:T(8,128)}) %reduce-scatter.2.cloned.1.call-update) | async-done | bytes 393232 | tf_op jit(solution)/shard_map/reduce_scatter | solution.py:52
  368.5 1.0 convert_element_type.24
  369.6 0.6 collective-permute-start
  370.2 5.1 %collective-permute-done = bf16[8,12288]{1,0:T(8,128)(2,1)S(1)} collective-permute-done((bf16[8,12288]{1,0:T(8,128)(2,1)S(1)}, bf16[8,12288]{1,0:T(8,128)(2,1)S(1)}, u32[]{:S(2)}, u32[]{:S(2)}) %collective-permute-start) | collective-permute-done | bytes 196640 | tf_op jit(solution)/shard_map/ppermute | solution.py:11
  375.3 0.7 copy.6
  (2 shorter events, 0.0 us)
Async XLA Ops:
  6.5 115.8 %copy-start = (bf16[1,128,12288]{2,1,0:T(8,128)(2,1)S(1)}, bf16[1,128,12288]{2,1,0:T(8,128)(2,1)}, u32[]{:S(2)}) copy-start(bf16[1,128,12288]{2,1,0:T(8,128)(2,1)} %param.7) | copy-start | bytes 9437188
  6.5 100.0 %all-gather.2.cloned.1.call-start = ((), (), s32[]{:S(2)}) async-start(), calls=%async_computation.1 | async-start | bytes 12779520 | tf_op jit(solution)/shard_map/all_gather | solution.py:46
  10.8 357.7 %reduce-scatter.2.cloned.1.call-start = ((), (), s32[]{:S(2)}) async-start(), calls=%async_computation.2 | async-start | bytes 25559040 | tf_op jit(solution)/shard_map/reduce_scatter | solution.py:52
  119.2 0.9 copy-start.2
  121.1 1.1 copy-start.1
  369.6 5.7 %collective-permute-start = (bf16[8,12288]{1,0:T(8,128)(2,1)S(1)}, bf16[8,12288]{1,0:T(8,128)(2,1)S(1)}, u32[]{:S(2)}, u32[]{:S(2)}) collective-permute-start(bf16[8,12288]{1,0:T(8,128)(2,1)S(1)} %convert_element_type.24), channel_id=1, source_target_pairs={{0,64},{64,0},{1,65},{65,1},{2,66},{66,2},{3,67},{67,3},{4,68},{68... | collective-permute-start | bytes 589832 | tf_op jit(solution)/shard_map/ppermute | solution.py:11
Sparse Core Ops, SparseCore 0:
  10.9 95.5 all-gather.1
  134.2 234.2 reduce-scatter.1
where the time goes:
time: 383 us
  waiting for transfers between devices  335 us (87%)
  matrix products  25.5 us (7%)
  between operations  13.4 us (3%)
  other arithmetic  5.42 us (1%)
    reduce_scatter x1, waiting for transfers between devices, shards(): lax.psum_scatter(jnp.dot(attended, out_rows, preferred_element_type=jnp.f...  234 us
    all_gather x1, waiting for transfers between devices, shards(): lax.all_gather(normed, 'dp', axis=0, tiled=True)  95.6 us
    dot_general x1, matrix products, shards(): jnp.dot(lax.all_gather(normed, 'dp', axis=0, tiled=True), head_block, pre...  12.7 us
    dot_general x1, matrix products, shards(): jnp.dot(attended, out_rows, preferred_element_type=jnp.float32)  11.8 us
  transfers between devices with their start and end apart: 3, of which 3 were waited for; matrix products, arithmetic and copies ran while one was open for 0% of the time, Pallas kernels for 0%

commit v1 on v0

--- a/solution.py
+++ b/solution.py
@@ -43,7 +43,9 @@
     normed = normalize(segment_input[0], norm_gain[0])
     head_block = head_weights[0, :, 0, :]
     projected = jnp.dot(
-        lax.all_gather(normed, "dp", axis=0, tiled=True),
+        jnp.concatenate(
+            lax.all_to_all(jnp.stack([normed] * lax.axis_size("dp")), "dp", 0, 0), axis=0
+        ),
         head_block,
         preferred_element_type=jnp.float32,
     )

time: 383 us -> 442 us (1.15)
  blocking collectives: 0 us -> 154 us
  waiting for transfers between devices: 335 us -> 239 us
  local copies, waits for them, and re-layouts: 2.63 us -> 8.71 us
    all_to_all x0 -> x1, blocking collectives: none -> 154 us  [shards(): lax.all_to_all(jnp.stack([normed] * lax.axis_size('dp')), 'dp', 0, 0)]
    all_gather x1 -> x0, waiting for transfers between devices: 95.6 us -> none  [shards(): lax.all_gather(normed, 'dp', axis=0, tiled=True)]
    another operation x0 -> x1, local copies, waits for them, and re-layouts: none -> 6.09 us  [shards(): jnp.stack([normed] * lax.axis_size('dp'))]
  transfers between devices with their start and end apart: 3 -> 2, of which waited for: 3 -> 2; matrix products, arithmetic and copies ran while one was open for 0% -> 0% of each run, Pallas kernels for 0% -> 0%
where the time goes in v1:
time: 442 us
  waiting for transfers between devices  239 us (54%)
  blocking collectives  154 us (35%)
  matrix products  22 us (5%)
  between operations  13.4 us (3%)
  local copies, waits for them, and re-layouts  8.71 us (2%)
  other arithmetic  4.74 us (1%)
    reduce_scatter x1, waiting for transfers between devices, shards(): lax.psum_scatter(jnp.dot(attended, out_rows, preferred_element_type=jnp.f...  233 us
    all_to_all x1, blocking collectives, shards(): lax.all_to_all(jnp.stack([normed] * lax.axis_size('dp')), 'dp', 0, 0)  154 us
    dot_general x1, matrix products, shards(): jnp.dot(attended, out_rows, preferred_element_type=jnp.float32)  11.8 us
    dot_general x1, matrix products, shards(): jnp.dot(jnp.concatenate(lax.all_to_all(jnp.stack([normed] * lax.axis_size...  9.23 us
  transfers between devices with their start and end apart: 2, of which 2 were waited for; matrix products, arithmetic and copies ran while one was open for 0% of the time, Pallas kernels for 0%

profile of v1, /device:TPU:0, one launch (start us, length us, event | category | flops | bytes accessed | tf_op | source)
XLA Modules:
  0.0 442.2 jit_solution(18158575977709054743)
XLA Ops:
  6.5 0.0 copy-start
  6.5 0.0 reduce-scatter.2.cloned.1.call-start
  6.5 1.3 convert_reduce_fusion
  7.8 1.2 fusion.18
  9.1 1.1 fusion.21
  10.1 6.1 %stack.5 = bf16[64,8,12288]{2,1,0:T(8,128)(2,1)} broadcast(bf16[8,12288]{1,0:T(8,128)(2,1)S(1)} %fusion.21), dimensions={1,2} | broadcast | bytes 12779520 | tf_op jit(solution)/shard_map/stack | solution.py:47
  16.2 154.0 %all_to_all.5 = bf16[64,8,12288]{2,1,0:T(8,128)(2,1)S(1)} all-to-all(bf16[64,8,12288]{2,1,0:T(8,128)(2,1)} %stack.5), channel_id=1, replica_groups=mesh['pipe'=2,'dp'=64] {'dp'}, dimensions={0} | all-to-all | bytes 25165824 | tf_op jit(solution)/shard_map/all_to_all | solution.py:47
  170.3 9.2 %fusion = f32[512,384]{1,0:T(8,128)S(1)} fusion(bf16[64,8,12288]{2,1,0:T(8,128)(2,1)S(1)} %all_to_all.5, bf16[1,12288,1,384]{3,1,2,0:T(8,128)(2,1)} %param.6), kind=kOutput, calls=%fused_computation | convolution fusion | flops 4831838208 | bytes 22806528 | tf_op jit(solution)/shard_map/dot_general | solution.py:45
  179.5 0.0 copy-start.2
  179.5 0.9 copy-done.2
  180.4 1.0 fusion.24
  181.4 0.0 copy-start.1
  181.4 1.1 copy-done.1
  182.5 0.2 fusion.6
  182.6 0.0 copy-done
  182.6 11.8 %fusion.3 = f32[512,12288]{1,0:T(8,128)} fusion(bf16[1,128,12288]{2,1,0:T(8,128)(2,1)S(1)} %copy-done, f32[512,512]{0,1:T(8,128)} %copy-done.1, f32[512]{0:T(512)S(1)} %fusion.6, f32[512]{0:T(512)S(1)} %get-tuple-element.5, f32[512,384]{1,0:T(8,128)} %copy-done.2), kind=kOutput, calls=%fused_computation.3 | convolution fusion | flops 1679097856 | bytes 29495296 | tf_op jit(solution)/shard_map/dot_general | solution.py:55
  194.4 0.0 reduce-scatter.2.cloned.1.call-update
  194.4 233.5 %reduce-scatter.2.cloned.1.call-done = f32[8,12288]{1,0:T(8,128)} async-done(((f32[512,12288]{1,0:T(8,128)}), f32[8,12288]{1,0:T(8,128)}) %reduce-scatter.2.cloned.1.call-update) | async-done | bytes 393232 | tf_op jit(solution)/shard_map/reduce_scatter | solution.py:54
  427.9 1.0 convert_element_type.26
  428.9 0.7 collective-permute-start
  429.5 5.1 %collective-permute-done = bf16[8,12288]{1,0:T(8,128)(2,1)S(1)} collective-permute-done((bf16[8,12288]{1,0:T(8,128)(2,1)S(1)}, bf16[8,12288]{1,0:T(8,128)(2,1)S(1)}, u32[]{:S(2)}, u32[]{:S(2)}) %collective-permute-start) | collective-permute-done | bytes 196640 | tf_op jit(solution)/shard_map/ppermute | solution.py:11
  434.6 0.7 copy.6
  (2 shorter events, 0.0 us)
Async XLA Ops:
  6.5 176.1 %copy-start = (bf16[1,128,12288]{2,1,0:T(8,128)(2,1)S(1)}, bf16[1,128,12288]{2,1,0:T(8,128)(2,1)}, u32[]{:S(2)}) copy-start(bf16[1,128,12288]{2,1,0:T(8,128)(2,1)} %param.7) | copy-start | bytes 9437188
  6.5 421.3 %reduce-scatter.2.cloned.1.call-start = ((), (), s32[]{:S(2)}) async-start(), calls=%async_computation.2 | async-start | bytes 25559040 | tf_op jit(solution)/shard_map/reduce_scatter | solution.py:54
  179.5 0.9 copy-start.2
  181.4 1.1 copy-start.1
  428.9 5.7 %collective-permute-start = (bf16[8,12288]{1,0:T(8,128)(2,1)S(1)}, bf16[8,12288]{1,0:T(8,128)(2,1)S(1)}, u32[]{:S(2)}, u32[]{:S(2)}) collective-permute-start(bf16[8,12288]{1,0:T(8,128)(2,1)S(1)} %convert_element_type.26), channel_id=1, source_target_pairs={{0,64},{64,0},{1,65},{65,1},{2,66},{66,2},{3,67},{67,3},{4,68},{68... | collective-permute-start | bytes 589832 | tf_op jit(solution)/shard_map/ppermute | solution.py:11
Sparse Core Ops, SparseCore 0:
  194.5 233.2 reduce-scatter.1
